TPU v7x, 32 devices: a whole 2x2x4 slice. The times are simulated.
32 devices in a mesh: row: 4 (over x, core), col: 8 (over z, y).
Axes of the slice: x: 2, y: 2, z: 4, core: 2. Of those that a mesh axis runs over, the one named last changes fastest.
Arguments:
- kernel: bfloat16 [32768, 32768], P('row', 'col'), may hold values from -1 to 1
- random_cols: bfloat16 [32768, 256], P('row'), may hold values from -6 to 6
- tree_perm: int32 [32768], replicated, may hold values from 0 to 32767, as said below
- leaf_units: int32 [32], replicated, may hold values from 1 to 8, 160 in all
Outputs:
- bases: bfloat16 [4, 32768, 256], P(None, ('row', 'col'))
Inputs may be any that keep to these rules, and one draw needn't show every extreme that they name: `tree_perm`: A permutation. Cut tree positions and stored rows alike into blocks of 1024 in order: every tree block takes at most 32 rows from any one stored block, some pair of blocks shares exactly 32, and every stored block gives 1024 rows in all. `leaf_units`: they sum to 160.
All inputs are finite; a program needn't handle non-finite values.
Results may differ from a plain program's by a relative error of at most 0.0067.
Values may be sent and summed in bfloat16 or wider, within the bound.
A program may use at most 192 MiB of HBM per device.

v0:
```python
import jax
import jax.numpy as jnp
from jax import lax
from jax.sharding import PartitionSpec as P

UNIT = 128
MINU = 4
LEVELS = 3


def shards(kernel, random_cols, tree_perm, leaf_units):
    width = random_cols.shape[1]
    partial_w = lax.dot_general(
        kernel, random_cols, (((0,), (0,)), ((), ())), preferred_element_type=jnp.float32
    )
    sample_w = lax.psum(partial_w, "row").astype(jnp.bfloat16)
    columns_count = lax.axis_size("col")
    rows_dev = kernel.shape[0] // columns_count
    sample = lax.psum_scatter(
        jnp.dot(kernel, sample_w, preferred_element_type=jnp.float32),
        "col",
        scatter_dimension=0,
        tiled=True,
    ).astype(jnp.bfloat16)
    devices = lax.axis_size("row") * columns_count
    total_rows = tree_perm.shape[0]
    device = lax.axis_index(("row", "col"))
    offset = device * rows_dev
    wanted = lax.dynamic_slice_in_dim(tree_perm, offset, rows_dev)
    inverse = (
        jnp.zeros((total_rows,), jnp.int32)
        .at[tree_perm]
        .set(jnp.arange(total_rows, dtype=jnp.int32))
    )
    placed = lax.dynamic_slice_in_dim(inverse, offset, rows_dev)
    capacity = (rows_dev + devices - 1) // devices
    target = placed // rows_dev
    ahead_mine = (target[None, :] == target[:, None]) & (placed[None, :] < placed[:, None])
    slot = target * capacity + jnp.sum(ahead_mine, axis=1)
    outgoing = jnp.zeros((devices * capacity, width), jnp.bfloat16).at[slot].set(sample)
    incoming = lax.all_to_all(outgoing, ("row", "col"), split_axis=0, concat_axis=0, tiled=True)
    source = wanted // rows_dev
    order = jnp.arange(rows_dev, dtype=jnp.int32)
    ahead_theirs = (source[None, :] == source[:, None]) & (order[None, :] < order[:, None])
    pick = source * capacity + jnp.sum(ahead_theirs, axis=1)
    tree_rows = jnp.take(incoming, pick, axis=0)
    sizes = UNIT * (MINU - 1 + leaf_units)
    leaves = sizes.shape[0]
    ends = jnp.cumsum(sizes)
    positions = offset + jnp.arange(rows_dev, dtype=jnp.int32)
    leaf_of = jnp.sum(positions[:, None] >= ends[None, :], axis=1)
    reach = rows_dev // (UNIT * MINU) + 2
    offsets = jnp.arange(reach, dtype=jnp.int32)
    levels = LEVELS + 1
    node_ids = [leaf_of // 2**level for level in range(levels)]
    totals = []
    stored_leaf = jnp.sum(placed[:, None] >= ends[None, :], axis=1)
    leaf_range = jnp.arange(leaves, dtype=jnp.int32)
    chosen = stored_leaf[None, :] == leaf_range[:, None]
    masked = jnp.where(chosen[:, :, None], sample[None, :, :], jnp.zeros((), jnp.bfloat16))
    spread = jnp.einsum("lrs,rt->lst", masked, sample, preferred_element_type=jnp.float32)
    leaf_grams = lax.psum(spread, ("row", "col"))
    for level in range(levels):
        group = 2**level
        count = leaves // group
        node_grams = leaf_grams.reshape(count, group, width, width).sum(axis=1)
        index = jnp.minimum(node_ids[level][0] + offsets, count - 1)
        totals.append(jnp.take(node_grams, index, axis=0))
    identity_matrix = jnp.eye(width, dtype=jnp.float32)
    values = tree_rows.astype(jnp.float32).T
    results = []
    for level in range(levels):
        ids = node_ids[level]
        group = 2**level
        count = leaves // group
        node_sizes = sizes.reshape(count, group).sum(axis=1)
        candidate = ids[0] + offsets
        present = candidate <= ids[-1]
        counts = jnp.take(node_sizes, jnp.minimum(candidate, count - 1)).astype(jnp.float32)
        mean = jnp.where(
            present[:, None, None], totals[level] / counts[:, None, None], identity_matrix[None]
        )
        factor = jnp.linalg.cholesky(mean)
        basis = jnp.zeros((rows_dev, width), jnp.float32)
        for which in range(reach):
            solved = jax.scipy.linalg.solve_triangular(factor[which], values, lower=True).T
            basis = basis + jnp.where((ids == candidate[which])[:, None], solved, 0.0)
        results.append(basis.astype(jnp.bfloat16))
    return jnp.stack(results)


def solution(mesh):
    return jax.shard_map(
        shards,
        mesh=mesh,
        in_specs=(P("row", "col"), P("row", None), P(), P()),
        out_specs=P(None, ("row", "col"), None),
        check_vma=False,
    )
```

profile of v0, /device:TPU:0, one launch (start us, length us, event | category | flops | bytes accessed | tf_op | source)
XLA Modules:
  0.0 1622.3 jit_solution(10285654006331508957)
XLA Ops:
  6.5 30.1 %fusion.169 = f32[4096,256]{1,0:T(8,128)} fusion(bf16[8192,4096]{1,0:T(8,128)(2,1)} %param.7, bf16[8192,256]{1,0:T(8,128)(2,1)} %param.8), kind=kOutput, calls=%fused_computation.425 | convolution fusion | flops 17179869184 | bytes 75497472 | tf_op jit(solution)/shard_map/dot_general | solution.py:13
  36.6 78.7 %all-reduce.5 = bf16[4096,256]{1,0:T(8,128)(2,1)S(1)} all-reduce(f32[4096,256]{1,0:T(8,128)} %fusion.169), channel_id=1, replica_groups=mesh['row'=4,'col'=8] {'row'}, use_global_device_ids=true, to_apply=%region_4.5 | all-reduce | flops 1048576 | bytes 6291456 | tf_op jit(solution)/shard_map/psum | solution.py:16
  115.4 30.2 %convolution_bitcast_fusion = f32[8192,256]{0,1:T(8,128)} fusion(bf16[8192,4096]{1,0:T(8,128)(2,1)} %param.7, bf16[4096,256]{1,0:T(8,128)(2,1)S(1)} %all-reduce.5), kind=kOutput, calls=%fused_computation.46 | convolution fusion | flops 17179869184 | bytes 77594624 | tf_op jit(solution)/shard_map/dot_general | solution.py:20
  146.5 120.1 %scatter_custom_fusion = s32[32768]{0:T(1024)S(1)} fusion(s32[32768]{0:T(1024)S(1)} %compare_select_fusion, s32[32768]{0:T(1024)S(1)} %iota.124, s32[]{:T(128)} %copy.190), kind=kCustom, calls=%fused_computation.279 | custom fusion | bytes 131076 | tf_op jit(solution)/shard_map/scatter | solution.py:33
  359.0 131.6 %all-reduce.4.cloned.1.call-done = f32[32,256,256]{2,1,0:T(8,128)} async-done(((f32[32,256,256]{2,1,0:T(8,128)}), f32[32,256,256]{2,1,0:T(8,128)}) %all-reduce.4.cloned.1.call-update) | async-done | bytes 8388624 | tf_op jit(solution)/shard_map/psum | solution.py:62
  531.1 47.7 %custom-call.37 = f32[4,128,128]{2,1,0:T(8,128)S(1)} custom-call(f32[4,128,128]{2,1,0:T(8,128)} %cholesky.350), custom_call_target="Cholesky" | custom-call | tf_op jit(solution)/shard_map/jit(cholesky)/cholesky | solution.py:83
  584.8 48.5 %custom-call.51 = f32[4,128,128]{2,1,0:T(8,128)} custom-call(f32[4,128,128]{2,1,0:T(8,128)} %cholesky.356), custom_call_target="Cholesky" | custom-call | tf_op jit(solution)/shard_map/jit(cholesky)/cholesky | solution.py:83
  637.0 47.5 %custom-call.44 = f32[4,128,128]{2,1,0:T(8,128)} custom-call(f32[4,128,128]{2,1,0:T(8,128)S(1)} %cholesky.353), custom_call_target="Cholesky" | custom-call | tf_op jit(solution)/shard_map/jit(cholesky)/cholesky | solution.py:83
  686.0 47.3 %custom-call.58 = f32[4,128,128]{2,1,0:T(8,128)S(1)} custom-call(f32[4,128,128]{2,1,0:T(8,128)S(1)} %cholesky.359), custom_call_target="Cholesky" | custom-call | tf_op jit(solution)/shard_map/jit(cholesky)/cholesky | solution.py:83
  735.4 39.3 %custom-call.38 = f32[4,1,128,128]{2,3,1,0:T(8,128)S(1)} custom-call(f32[4,1,128,128]{3,2,1,0:T(8,128)S(1)} %get-tuple-element.324), custom_call_target="InvertDiagBlocksLowerTriangular" | custom-call | tf_op jit(solution)/shard_map/jit(cholesky)/cholesky | solution.py:83
  777.7 47.5 %custom-call.39 = f32[4,128,128]{2,1,0:T(8,128)} custom-call(f32[4,128,128]{2,1,0:T(8,128)S(1)} %convolution_subtract_fusion.19), custom_call_target="Cholesky" | custom-call | tf_op jit(solution)/shard_map/jit(cholesky)/cholesky | solution.py:83
  826.3 40.9 %custom-call.45 = f32[4,1,128,128]{2,3,1,0:T(8,128)} custom-call(f32[4,1,128,128]{3,2,1,0:T(8,128)} %get-tuple-element.322), custom_call_target="InvertDiagBlocksLowerTriangular" | custom-call | tf_op jit(solution)/shard_map/jit(cholesky)/cholesky | solution.py:83
  871.2 48.3 %custom-call.46 = f32[4,128,128]{2,1,0:T(8,128)} custom-call(f32[4,128,128]{2,1,0:T(8,128)} %convolution_subtract_fusion.18), custom_call_target="Cholesky" | custom-call | tf_op jit(solution)/shard_map/jit(cholesky)/cholesky | solution.py:83
  921.6 40.7 %custom-call.52 = f32[4,1,128,128]{2,3,1,0:T(8,128)} custom-call(f32[4,1,128,128]{3,2,1,0:T(8,128)} %get-tuple-element.321), custom_call_target="InvertDiagBlocksLowerTriangular" | custom-call | tf_op jit(solution)/shard_map/jit(cholesky)/cholesky | solution.py:83
  966.8 48.5 %custom-call.53 = f32[4,128,128]{2,1,0:T(8,128)} custom-call(f32[4,128,128]{2,1,0:T(8,128)} %convolution_subtract_fusion.17), custom_call_target="Cholesky" | custom-call | tf_op jit(solution)/shard_map/jit(cholesky)/cholesky | solution.py:83
  1016.4 40.8 %custom-call.59 = f32[4,1,128,128]{2,3,1,0:T(8,128)} custom-call(f32[4,1,128,128]{3,2,1,0:T(8,128)} %get-tuple-element.323), custom_call_target="InvertDiagBlocksLowerTriangular" | custom-call | tf_op jit(solution)/shard_map/jit(cholesky)/cholesky | solution.py:83
  1060.9 48.3 %custom-call.60 = f32[4,128,128]{2,1,0:T(8,128)} custom-call(f32[4,128,128]{2,1,0:T(8,128)} %convolution_subtract_fusion.16), custom_call_target="Cholesky" | custom-call | tf_op jit(solution)/shard_map/jit(cholesky)/cholesky | solution.py:83
  1264.4 20.5 %custom-call.56 = f32[2,128,128]{1,2,0:T(8,128)S(1)} custom-call(f32[2,128,128]{2,1,0:T(8,128)} %copy-done.48), custom_call_target="InvertDiagBlocksLowerTriangular" | custom-call | tf_op jit(solution)/shard_map/jit(_solve_triangular)/triangular_solve | solution.py:86
  1297.0 20.7 %custom-call.55 = f32[2,128,128]{1,2,0:T(8,128)S(1)} custom-call(f32[2,128,128]{2,1,0:T(8,128)} %copy-done.49), custom_call_target="InvertDiagBlocksLowerTriangular" | custom-call | tf_op jit(solution)/shard_map/jit(_solve_triangular)/triangular_solve | solution.py:86
  1360.4 20.5 %custom-call.50 = f32[2,128,128]{1,2,0:T(8,128)S(1)} custom-call(f32[2,128,128]{2,1,0:T(8,128)} %copy-done.51), custom_call_target="InvertDiagBlocksLowerTriangular" | custom-call | tf_op jit(solution)/shard_map/jit(_solve_triangular)/triangular_solve | solution.py:86
  1392.7 20.9 %custom-call.49 = f32[2,128,128]{1,2,0:T(8,128)S(1)} custom-call(f32[2,128,128]{2,1,0:T(8,128)} %copy-done.52), custom_call_target="InvertDiagBlocksLowerTriangular" | custom-call | tf_op jit(solution)/shard_map/jit(_solve_triangular)/triangular_solve | solution.py:86
  1456.6 20.5 %custom-call.47 = f32[2,128,128]{1,2,0:T(8,128)S(1)} custom-call(f32[2,128,128]{2,1,0:T(8,128)} %copy-done.54), custom_call_target="InvertDiagBlocksLowerTriangular" | custom-call | tf_op jit(solution)/shard_map/jit(_solve_triangular)/triangular_solve | solution.py:86
  1489.4 20.6 %custom-call.43 = f32[2,128,128]{1,2,0:T(8,128)S(1)} custom-call(f32[2,128,128]{2,1,0:T(8,128)} %copy-done.55), custom_call_target="InvertDiagBlocksLowerTriangular" | custom-call | tf_op jit(solution)/shard_map/jit(_solve_triangular)/triangular_solve | solution.py:86
  1585.2 20.7 %custom-call.40 = f32[2,128,128]{1,2,0:T(8,128)S(1)} custom-call(f32[2,128,128]{2,1,0:T(8,128)} %copy-done.46), custom_call_target="InvertDiagBlocksLowerTriangular" | custom-call | tf_op jit(solution)/shard_map/jit(_solve_triangular)/triangular_solve | solution.py:86
  (466 shorter events, 621.0 us)
Async XLA Ops:
  6.5 287.5 %reduce-scatter.2.cloned.1.call-start = ((), (), s32[]{:S(2)}) async-start(), calls=%async_computation.2 | async-start | bytes 9437184 | tf_op jit(solution)/shard_map/reduce_scatter | solution.py:19
  145.6 345.1 %all-reduce.4.cloned.1.call-start = ((), (), s32[]{:S(2)}) async-start(), calls=%async_computation.3 | async-start | bytes 16777216 | tf_op jit(solution)/shard_map/psum | solution.py:62
  329.1 25.7 %all-to-all-start = ((bf16[32,32,256]{2,1,0:T(8,128)(2,1)}), bf16[32,32,256]{2,1,0:T(8,128)(2,1)S(1)}, u32[]{:S(2)}, u32[]{:S(2)}) async-start(bf16[32,32,256]{2,1,0:T(8,128)(2,1)} %bitcast.13), calls=%async_computation.1 | async-start | bytes 1048576 | tf_op jit(solution)/shard_map/all_to_all | solution.py:41
  513.7 7.3 copy-start.66
  513.7 7.3 copy-start.67
  514.4 6.7 copy-start.68
  733.3 44.4 %copy-start.30 = (f32[4,128,128]{2,1,0:T(8,128)}, f32[4,128,128]{2,1,0:T(8,128)S(1)}, u32[]{:S(2)}) copy-start(f32[4,128,128]{2,1,0:T(8,128)S(1)} %custom-call.58) | copy-start | bytes 786436
  868.7 98.1 %copy-start.25 = (f32[4,256,256]{2,1,0:T(8,128)}, f32[4,256,256]{2,1,0:T(8,128)S(1)}, u32[]{:S(2)}) copy-start(f32[4,256,256]{2,1,0:T(8,128)S(1)} %get-tuple-element.372) | copy-start | bytes 3145732
  1112.6 3.6 copy-start.71
  1220.5 2.7 copy-start.24
  1348.5 3.5 copy-start.23
  1477.1 3.5 copy-start.22
  1606.0 3.9 copy-start.1
  1606.0 3.9 copy-start.3
  1606.0 3.9 copy-start.5
  1606.0 3.9 copy-start.7
  1606.0 3.9 copy-start.34
  1606.0 3.9 copy-start.35
  1606.0 3.9 copy-start.36
  1606.0 3.9 copy-start.37
  1606.0 3.9 copy-start.62
  1606.0 3.9 copy-start.63
  1606.1 3.9 copy-start.64
  1606.1 3.9 copy-start.65
  (51 other events, 69.0 us)
Sparse Core Ops, SparseCore 0:
  145.7 148.2 reduce-scatter.1
  302.2 188.3 all-reduce.3
where the time goes:
time: 1630 us; the launch traced here: 1620 us
  other arithmetic  944 us (58%)
  local copies, waits for them, and re-layouts  286 us (18%)
  waiting for transfers between devices  162 us (10%)
  matrix products  131 us (8%)
  blocking collectives  78.7 us (5%)
    another operation x28, other arithmetic, shards(): factor = jnp.linalg.cholesky(mean)  551 us
    another operation x22, other arithmetic, shards(): jax.scipy.linalg.solve_triangular(factor[which], values, lower=True)  329 us
    psum x1, waiting for transfers between devices, shards(): leaf_grams = lax.psum(spread, ('row', 'col'))  132 us
    scatter x1, local copies, waits for them, and re-layouts, shards(): inverse = jnp.zeros((total_rows,), jnp.int32).at[tree_perm].set(jnp.arang...  120 us
    another operation x113, local copies, waits for them, and re-layouts, shards(): jax.scipy.linalg.solve_triangular(factor[which], values, lower=True)  95 us
    psum x1, blocking collectives, shards(): sample_w = lax.psum(partial_w, 'row').astype(jnp.bfloat16)  78.7 us
    another operation x48, matrix products, shards(): jax.scipy.linalg.solve_triangular(factor[which], values, lower=True)  49.2 us
  transfers between devices with their start and end apart: 3, of which 3 were waited for; matrix products, arithmetic and copies ran while one was open for 11% of the time, Pallas kernels for 0%

commit v1 on v0

--- a/solution.py
+++ b/solution.py
@@ -59,7 +59,7 @@
     chosen = stored_leaf[None, :] == leaf_range[:, None]
     masked = jnp.where(chosen[:, :, None], sample[None, :, :], jnp.zeros((), jnp.bfloat16))
     spread = jnp.einsum("lrs,rt->lst", masked, sample, preferred_element_type=jnp.float32)
-    leaf_grams = lax.psum(spread, ("row", "col"))
+    leaf_grams = lax.psum(lax.psum(spread, "col"), "row")
     for level in range(levels):
         group = 2**level
         count = leaves // group

time: 1630 us -> 1870 us (1.15)
  waiting for transfers between devices: 162 us -> 402 us
    psum x1 -> x2, waiting for transfers between devices: 132 us -> 370 us  [shards(): leaf_grams = lax.psum(lax.psum(spread, 'col'), 'row')]
  transfers between devices with their start and end apart: 3 -> 4, of which waited for: 3 -> 4; matrix products, arithmetic and copies ran while one was open for 11% -> 9% of each run, Pallas kernels for 0% -> 0%
where the time goes in v1:
time: 1870 us; the launch traced here: 1860 us
  other arithmetic  945 us (51%)
  waiting for transfers between devices  402 us (21%)
  local copies, waits for them, and re-layouts  286 us (15%)
  matrix products  131 us (7%)
  blocking collectives  78.7 us (4%)
    another operation x28, other arithmetic, shards(): factor = jnp.linalg.cholesky(mean)  551 us
    psum x2, waiting for transfers between devices, shards(): leaf_grams = lax.psum(lax.psum(spread, 'col'), 'row')  370 us
    another operation x22, other arithmetic, shards(): jax.scipy.linalg.solve_triangular(factor[which], values, lower=True)  329 us
    scatter x1, local copies, waits for them, and re-layouts, shards(): inverse = jnp.zeros((total_rows,), jnp.int32).at[tree_perm].set(jnp.arang...  120 us
    another operation x113, local copies, waits for them, and re-layouts, shards(): jax.scipy.linalg.solve_triangular(factor[which], values, lower=True)  95 us
    psum x1, blocking collectives, shards(): sample_w = lax.psum(partial_w, 'row').astype(jnp.bfloat16)  78.7 us
    another operation x48, matrix products, shards(): jax.scipy.linalg.solve_triangular(factor[which], values, lower=True)  49.2 us
  transfers between devices with their start and end apart: 4, of which 4 were waited for; matrix products, arithmetic and copies ran while one was open for 9% of the time, Pallas kernels for 0%

profile of v1, /device:TPU:0, one launch (start us, length us, event | category | flops | bytes accessed | tf_op | source)
XLA Modules:
  0.0 1862.8 jit_solution(17802566809061573151)
XLA Ops:
  6.5 30.1 %fusion.169 = f32[4096,256]{1,0:T(8,128)} fusion(bf16[8192,4096]{1,0:T(8,128)(2,1)} %param.7, bf16[8192,256]{1,0:T(8,128)(2,1)} %param.8), kind=kOutput, calls=%fused_computation.425 | convolution fusion | flops 17179869184 | bytes 75497472 | tf_op jit(solution)/shard_map/dot_general | solution.py:13
  36.6 78.7 %all-reduce.8 = bf16[4096,256]{1,0:T(8,128)(2,1)S(1)} all-reduce(f32[4096,256]{1,0:T(8,128)} %fusion.169), channel_id=1, replica_groups=mesh['row'=4,'col'=8] {'row'}, use_global_device_ids=true, to_apply=%region_4.5 | all-reduce | flops 1048576 | bytes 6291456 | tf_op jit(solution)/shard_map/psum | solution.py:16
  115.4 30.2 %convolution_bitcast_fusion = f32[8192,256]{0,1:T(8,128)} fusion(bf16[8192,4096]{1,0:T(8,128)(2,1)} %param.7, bf16[4096,256]{1,0:T(8,128)(2,1)S(1)} %all-reduce.8), kind=kOutput, calls=%fused_computation.46 | convolution fusion | flops 17179869184 | bytes 77594624 | tf_op jit(solution)/shard_map/dot_general | solution.py:20
  146.5 120.1 %scatter_custom_fusion = s32[32768]{0:T(1024)S(1)} fusion(s32[32768]{0:T(1024)S(1)} %compare_select_fusion, s32[32768]{0:T(1024)S(1)} %iota.124, s32[]{:T(128)} %copy.191), kind=kCustom, calls=%fused_computation.279 | custom fusion | bytes 131076 | tf_op jit(solution)/shard_map/scatter | solution.py:33
  266.8 27.2 %reduce-scatter.2.cloned.1.call-done = f32[1024,256]{0,1:T(8,128)} async-done(((f32[8192,256]{0,1:T(8,128)}), f32[1024,256]{0,1:T(8,128)}) %reduce-scatter.2.cloned.1.call-update) | async-done | bytes 1048592 | tf_op jit(solution)/shard_map/reduce_scatter | solution.py:19
  312.3 259.1 %all-reduce.5.cloned.1.call-done = f32[32,256,256]{2,1,0:T(8,128)} async-done(((f32[32,256,256]{2,1,0:T(8,128)}), f32[32,256,256]{2,1,0:T(8,128)}) %all-reduce.5.cloned.1.call-update) | async-done | bytes 8388624 | tf_op jit(solution)/shard_map/psum | solution.py:62
  620.8 110.7 %all-reduce.7.cloned.1.call-done = f32[32,256,256]{2,1,0:T(8,128)} async-done(((f32[32,256,256]{2,1,0:T(8,128)}), f32[32,256,256]{2,1,0:T(8,128)}) %all-reduce.7.cloned.1.call-update) | async-done | bytes 8388624 | tf_op jit(solution)/shard_map/psum | solution.py:62
  771.9 47.7 %custom-call.37 = f32[4,128,128]{2,1,0:T(8,128)S(1)} custom-call(f32[4,128,128]{2,1,0:T(8,128)} %cholesky.350), custom_call_target="Cholesky" | custom-call | tf_op jit(solution)/shard_map/jit(cholesky)/cholesky | solution.py:83
  825.6 48.5 %custom-call.51 = f32[4,128,128]{2,1,0:T(8,128)} custom-call(f32[4,128,128]{2,1,0:T(8,128)} %cholesky.356), custom_call_target="Cholesky" | custom-call | tf_op jit(solution)/shard_map/jit(cholesky)/cholesky | solution.py:83
  877.8 47.5 %custom-call.44 = f32[4,128,128]{2,1,0:T(8,128)} custom-call(f32[4,128,128]{2,1,0:T(8,128)S(1)} %cholesky.353), custom_call_target="Cholesky" | custom-call | tf_op jit(solution)/shard_map/jit(cholesky)/cholesky | solution.py:83
  926.8 47.3 %custom-call.58 = f32[4,128,128]{2,1,0:T(8,128)S(1)} custom-call(f32[4,128,128]{2,1,0:T(8,128)S(1)} %cholesky.359), custom_call_target="Cholesky" | custom-call | tf_op jit(solution)/shard_map/jit(cholesky)/cholesky | solution.py:83
  976.2 39.3 %custom-call.38 = f32[4,1,128,128]{2,3,1,0:T(8,128)S(1)} custom-call(f32[4,1,128,128]{3,2,1,0:T(8,128)S(1)} %get-tuple-element.324), custom_call_target="InvertDiagBlocksLowerTriangular" | custom-call | tf_op jit(solution)/shard_map/jit(cholesky)/cholesky | solution.py:83
  1018.5 47.5 %custom-call.39 = f32[4,128,128]{2,1,0:T(8,128)} custom-call(f32[4,128,128]{2,1,0:T(8,128)S(1)} %convolution_subtract_fusion.19), custom_call_target="Cholesky" | custom-call | tf_op jit(solution)/shard_map/jit(cholesky)/cholesky | solution.py:83
  1067.1 40.9 %custom-call.45 = f32[4,1,128,128]{2,3,1,0:T(8,128)} custom-call(f32[4,1,128,128]{3,2,1,0:T(8,128)} %get-tuple-element.322), custom_call_target="InvertDiagBlocksLowerTriangular" | custom-call | tf_op jit(solution)/shard_map/jit(cholesky)/cholesky | solution.py:83
  1112.0 48.3 %custom-call.46 = f32[4,128,128]{2,1,0:T(8,128)} custom-call(f32[4,128,128]{2,1,0:T(8,128)} %convolution_subtract_fusion.18), custom_call_target="Cholesky" | custom-call | tf_op jit(solution)/shard_map/jit(cholesky)/cholesky | solution.py:83
  1162.4 40.7 %custom-call.52 = f32[4,1,128,128]{2,3,1,0:T(8,128)} custom-call(f32[4,1,128,128]{3,2,1,0:T(8,128)} %get-tuple-element.321), custom_call_target="InvertDiagBlocksLowerTriangular" | custom-call | tf_op jit(solution)/shard_map/jit(cholesky)/cholesky | solution.py:83
  1207.6 48.5 %custom-call.53 = f32[4,128,128]{2,1,0:T(8,128)} custom-call(f32[4,128,128]{2,1,0:T(8,128)} %convolution_subtract_fusion.17), custom_call_target="Cholesky" | custom-call | tf_op jit(solution)/shard_map/jit(cholesky)/cholesky | solution.py:83
  1257.2 40.8 %custom-call.59 = f32[4,1,128,128]{2,3,1,0:T(8,128)} custom-call(f32[4,1,128,128]{3,2,1,0:T(8,128)} %get-tuple-element.323), custom_call_target="InvertDiagBlocksLowerTriangular" | custom-call | tf_op jit(solution)/shard_map/jit(cholesky)/cholesky | solution.py:83
  1301.7 48.3 %custom-call.60 = f32[4,128,128]{2,1,0:T(8,128)} custom-call(f32[4,128,128]{2,1,0:T(8,128)} %convolution_subtract_fusion.16), custom_call_target="Cholesky" | custom-call | tf_op jit(solution)/shard_map/jit(cholesky)/cholesky | solution.py:83
  1505.1 20.5 %custom-call.56 = f32[2,128,128]{1,2,0:T(8,128)S(1)} custom-call(f32[2,128,128]{2,1,0:T(8,128)} %copy-done.48), custom_call_target="InvertDiagBlocksLowerTriangular" | custom-call | tf_op jit(solution)/shard_map/jit(_solve_triangular)/triangular_solve | solution.py:86
  1537.8 20.7 %custom-call.55 = f32[2,128,128]{1,2,0:T(8,128)S(1)} custom-call(f32[2,128,128]{2,1,0:T(8,128)} %copy-done.49), custom_call_target="InvertDiagBlocksLowerTriangular" | custom-call | tf_op jit(solution)/shard_map/jit(_solve_triangular)/triangular_solve | solution.py:86
  1633.5 20.9 %custom-call.49 = f32[2,128,128]{1,2,0:T(8,128)S(1)} custom-call(f32[2,128,128]{2,1,0:T(8,128)} %copy-done.52), custom_call_target="InvertDiagBlocksLowerTriangular" | custom-call | tf_op jit(solution)/shard_map/jit(_solve_triangular)/triangular_solve | solution.py:86
  1730.1 20.6 %custom-call.43 = f32[2,128,128]{1,2,0:T(8,128)S(1)} custom-call(f32[2,128,128]{2,1,0:T(8,128)} %copy-done.55), custom_call_target="InvertDiagBlocksLowerTriangular" | custom-call | tf_op jit(solution)/shard_map/jit(_solve_triangular)/triangular_solve | solution.py:86
  1826.0 20.7 %custom-call.40 = f32[2,128,128]{1,2,0:T(8,128)S(1)} custom-call(f32[2,128,128]{2,1,0:T(8,128)} %copy-done.46), custom_call_target="InvertDiagBlocksLowerTriangular" | custom-call | tf_op jit(solution)/shard_map/jit(_solve_triangular)/triangular_solve | solution.py:86
  (469 shorter events, 637.4 us)
Async XLA Ops:
  6.5 287.5 %reduce-scatter.2.cloned.1.call-start = ((), (), s32[]{:S(2)}) async-start(), calls=%async_computation.2 | async-start | bytes 9437184 | tf_op jit(solution)/shard_map/reduce_scatter | solution.py:19
  145.6 425.7 %all-reduce.5.cloned.1.call-start = ((), (), s32[]{:S(2)}) async-start(), calls=%async_computation.3 | async-start | bytes 16777216 | tf_op jit(solution)/shard_map/psum | solution.py:62
  302.1 429.3 %all-reduce.7.cloned.1.call-start = ((), (), s32[]{:S(2)}) async-start(), calls=%async_computation.4 | async-start | bytes 16777216 | tf_op jit(solution)/shard_map/psum | solution.py:62
  596.4 20.1 %all-to-all-start = ((bf16[32,32,256]{2,1,0:T(8,128)(2,1)}), bf16[32,32,256]{2,1,0:T(8,128)(2,1)S(1)}, u32[]{:S(2)}, u32[]{:S(2)}) async-start(bf16[32,32,256]{2,1,0:T(8,128)(2,1)} %bitcast.13), calls=%async_computation.1 | async-start | bytes 1048576 | tf_op jit(solution)/shard_map/all_to_all | solution.py:41
  754.5 7.3 copy-start.66
  754.5 7.3 copy-start.67
  755.1 6.7 copy-start.68
  974.1 44.4 %copy-start.30 = (f32[4,128,128]{2,1,0:T(8,128)}, f32[4,128,128]{2,1,0:T(8,128)S(1)}, u32[]{:S(2)}) copy-start(f32[4,128,128]{2,1,0:T(8,128)S(1)} %custom-call.58) | copy-start | bytes 786436
  1109.4 98.1 %copy-start.25 = (f32[4,256,256]{2,1,0:T(8,128)}, f32[4,256,256]{2,1,0:T(8,128)S(1)}, u32[]{:S(2)}) copy-start(f32[4,256,256]{2,1,0:T(8,128)S(1)} %get-tuple-element.372) | copy-start | bytes 3145732
  1353.4 3.6 copy-start.71
  1589.3 3.5 copy-start.23
  1717.9 3.5 copy-start.22
  1846.7 3.9 copy-start.1
  1846.7 3.9 copy-start.3
  1846.8 3.9 copy-start.5
  1846.8 3.9 copy-start.7
  1846.8 3.9 copy-start.34
  1846.8 3.9 copy-start.35
  1846.8 3.9 copy-start.36
  1846.8 3.9 copy-start.37
  1846.8 3.9 copy-start.62
  1846.8 3.9 copy-start.63
  1846.8 3.9 copy-start.64
  1846.8 3.9 copy-start.65
  (52 other events, 71.7 us)
Sparse Core Ops, SparseCore 0:
  145.7 148.2 reduce-scatter.1
  302.2 269.0 all-reduce.4
  573.8 157.5 all-reduce.6
